TPU v7x, 32 devices: a whole 2x2x4 slice. The times are simulated.
32 devices in a mesh: group: 2 (over y), space: 4 (over x, core), src: 4 (over z).
Axes of the slice: x: 2, y: 2, z: 4, core: 2. Of those that a mesh axis runs over, the one named last changes fastest.
Arguments:
- conductivity: float32 [128, 32, 128], P(('group', 'space')), parts along dimension 0, may hold values from 0.2 to 5
- prior_potential: float32 [8, 64, 32, 128], P(('group', 'src'), 'space'), parts along dimension 0, may hold values from -6 to 6
- electrodes: int32 [8, 2], P(('group', 'src')), parts along dimension 0, may hold values from 0 to 262143
- currents: float32 [8], P(('group', 'src')), parts along dimension 0, may hold values from 2 to 20
- receivers: int32 [512], P('group'), parts along dimension 0, may hold values from 0 to 262143
- observed: float32 [8, 256], P(('group', 'src')), parts along dimension 0, may hold values from -3 to 3
Outputs:
- potential: float32 [8, 64, 32, 128], P(('group', 'src'), 'space'), parts along dimension 0
- misfit: float32 [8, 256], P(('group', 'src')), parts along dimension 0
- gradient: float32 [128, 32, 128], P(('group', 'space')), parts along dimension 0
There are 2 independent parts, one for each index of `group`. A program takes and returns all parts, laid end to end along the dimension named above; each array names one. Nothing has to cross between parts.
Inputs may be any that keep to these rules, and one draw needn't show every extreme that they name: Flat cell indices x * 32 * 128 + y * 128 + z; a source's two electrodes may fall in any cells. Flat cell indices as for electrodes; two receivers may share a cell.
All inputs are finite; a program needn't handle non-finite values.
Results may differ from a plain program's by a relative error of at most 0.0003.
Values sent between devices are 32-bit elements; how exact they have to be, the bound alone decides.
No kernel may reach another device: no remote copies, remote signals or barrier semaphores. Data moves between devices by JAX's collectives and lax.ppermute only.
A program may use at most 128 MiB of HBM per device.

v0:
```python
import jax
import jax.numpy as jnp
from jax import lax
from jax.sharding import PartitionSpec as P

LEVELS = 4
COARSE_SWEEPS = 4
OFFSETS = ((1, 0, 0), (-1, 0, 0), (0, 1, 0), (0, -1, 0), (0, 0, 1), (0, 0, -1))


def padded_2(block, sides, width):
    for axis, dim in sides:
        count = lax.axis_size(axis)
        forward = [(i, i + 1) for i in range(count - 1)]
        backward = [(target, source) for source, target in forward]
        low = lax.ppermute(
            lax.slice_in_dim(block, block.shape[dim] - width, None, axis=dim), axis, forward
        )
        high = lax.ppermute(lax.slice_in_dim(block, 0, width, axis=dim), axis, backward)
        block = jnp.concatenate([low, block, high], axis=dim)
    return block


def shifted(array, step):
    size_x, size_y, size_z = array.shape[-3:]
    return array[
        ...,
        1 + step[0] : size_x - 1 + step[0],
        1 + step[1] : size_y - 1 + step[1],
        1 + step[2] : size_z - 1 + step[2],
    ]


def couplings(sigma_ext, weight):
    padded = jnp.pad(sigma_ext, ((0, 0), (1, 1), (1, 1)))
    centre = shifted(padded, (0, 0, 0))
    return [weight * 0.5 * (centre + shifted(padded, step)) for step in OFFSETS]


def diagonal_of(coupled):
    summed = coupled[0]
    for coupling in coupled[1:]:
        summed = summed + coupling
    return summed


def neighbours(field_ext, coupled):
    padded = jnp.pad(field_ext, ((0, 0), (0, 0), (1, 1), (1, 1)))
    summed = coupled[0] * shifted(padded, OFFSETS[0])
    for coupling, step in zip(coupled[1:], OFFSETS[1:]):
        summed = summed + coupling * shifted(padded, step)
    return summed


def relax(field_ext, right_side, coupled, diagonal, colour_mask):
    update = (right_side + neighbours(field_ext, coupled)) / diagonal
    return jnp.where(colour_mask, update, field_ext[:, 1:-1])


def parity(planes, cells_y, cells_z, first_plane):
    plane_x = first_plane + lax.iota(jnp.int32, planes)
    plane_y = lax.iota(jnp.int32, cells_y)
    plane_z = lax.iota(jnp.int32, cells_z)
    summed = plane_x[:, None, None] + plane_y[None, :, None] + plane_z[None, None, :]
    return summed % 2 == 0


def boundary_planes(field_now, width):
    return padded_2(field_now, (("space", 1),), width)


def coarsen(array):
    size_x, size_y, size_z = array.shape[-3:]
    leading = array.shape[:-3]
    blocks = array.reshape(leading + (size_x // 2, 2, size_y // 2, 2, size_z // 2, 2))
    return blocks.mean(axis=(-5, -3, -1))


def refine(array):
    return jnp.repeat(jnp.repeat(jnp.repeat(array, 2, axis=-3), 2, axis=-2), 2, axis=-1)


def pairing(forward_ext, adjoint_ext):
    forward_mid = shifted(forward_ext, (0, 0, 0))
    adjoint_mid = shifted(adjoint_ext, (0, 0, 0))
    summed = jnp.zeros(forward_mid.shape, jnp.float32)
    for step in OFFSETS:
        summed = summed + (forward_mid - shifted(forward_ext, step)) * (
            adjoint_mid - shifted(adjoint_ext, step)
        )
    return -0.5 * jnp.sum(summed, axis=0)


def sweep_plain(field_now, right_side, grid_level, from_zero, extend):
    coupled, diagonal, red_mask = (grid_level[0], grid_level[1], grid_level[2])
    if from_zero:
        field_now = jnp.where(red_mask, right_side / diagonal, 0.0)
    else:
        field_now = relax(extend(field_now, 1), right_side, coupled, diagonal, red_mask)
    return relax(extend(field_now, 1), right_side, coupled, diagonal, jnp.logical_not(red_mask))


def smooth(field_now, right_side, grid_level, from_zero):
    return sweep_plain(field_now, right_side, grid_level, from_zero, boundary_planes)


def residual_of(field_now, right_side, grid_level):
    coupled, diagonal = (grid_level[0], grid_level[1])
    return right_side - (diagonal * field_now - neighbours(boundary_planes(field_now, 1), coupled))


def cycle(levels, level_index, right_side, field_now, from_zero):
    grid_level = levels[level_index]
    if level_index == len(levels) - 1:
        for sweep_index in range(COARSE_SWEEPS):
            field_now = smooth(field_now, right_side, grid_level, sweep_index == 0)
        return field_now
    field_now = smooth(field_now, right_side, grid_level, from_zero)
    coarse_rhs = coarsen(residual_of(field_now, right_side, grid_level))
    correction = cycle(levels, level_index + 1, coarse_rhs, None, True)
    field_now = field_now + refine(correction)
    return smooth(field_now, right_side, grid_level, False)


def body(conductivity, prior_potential, electrodes, currents, receivers, observed):
    rim_width = 1
    position = lax.axis_index("space")
    levels = []
    sigma_level = conductivity
    for level_index in range(LEVELS):
        planes, cells_y, cells_z = sigma_level.shape
        weight = 0.25**level_index
        extended = boundary_planes(sigma_level[None], rim_width)[0]
        coupled_all = couplings(extended, weight)
        red_mask = parity(planes, cells_y, cells_z, position * planes)
        levels.append((coupled_all, diagonal_of(coupled_all), red_mask, None, None, None))
        if level_index < LEVELS - 1:
            sigma_level = coarsen(sigma_level)
    sources, planes, cells_y, cells_z = prior_potential.shape
    cell_count = planes * cells_y * cells_z
    offset = position * cell_count

    def placed(flat_index):
        local_index = flat_index - offset
        return jnp.where((local_index >= 0) & (local_index < cell_count), local_index, cell_count)

    source_rows = jnp.arange(sources, dtype=jnp.int32)
    source = jnp.zeros((sources, cell_count), jnp.float32)
    source = source.at[source_rows, placed(electrodes[:, 0])].add(currents, mode="drop")
    source = source.at[source_rows, placed(electrodes[:, 1])].add(-currents, mode="drop")
    source = source.reshape(sources, planes, cells_y, cells_z)
    potential = cycle(levels, 0, source, prior_potential, False)
    local_index = receivers - offset
    inside_mask = (local_index >= 0) & (local_index < cell_count)
    picked = jnp.take(
        potential.reshape(sources, cell_count), jnp.clip(local_index, 0, cell_count - 1), axis=1
    )
    partial_values = jnp.where(inside_mask[None, :], picked, 0.0)
    at_receivers = lax.psum(partial_values, "space")
    misfit = at_receivers - observed
    adjoint_source = (
        jnp.zeros((sources, cell_count), jnp.float32)
        .at[:, placed(receivers)]
        .add(misfit, mode="drop")
    )
    adjoint = cycle(
        levels, 0, adjoint_source.reshape(sources, planes, cells_y, cells_z), None, True
    )
    stacked = boundary_planes(jnp.concatenate((potential, adjoint), 0), 1)
    stacked = jnp.pad(stacked, ((0, 0), (0, 0), (1, 1), (1, 1)))
    local_terms = pairing(stacked[:sources], stacked[sources:])
    gradient = lax.psum(local_terms, "src")
    return (potential, misfit, gradient)


def solution(mesh):
    return jax.shard_map(
        body,
        mesh=mesh,
        in_specs=(
            P(("group", "space"), None, None),
            P(("group", "src"), "space", None, None),
            P(("group", "src"), None),
            P(("group", "src")),
            P("group"),
            P(("group", "src"), None),
        ),
        out_specs=(
            P(("group", "src"), "space", None, None),
            P(("group", "src"), None),
            P(("group", "space"), None, None),
        ),
        check_vma=False,
    )
```

profile of v0, /device:TPU:0, one launch (start us, length us, event | category | flops | bytes accessed | tf_op | source)
XLA Modules:
  0.0 483.4 jit_solution(1726280062933962700)
XLA Ops:
  12.3 5.1 %collective-permute-start.3 = (f32[1,1,32,128]{3,2,1,0:T(8,128)S(1)}, f32[1,1,32,128]{3,2,1,0:T(8,128)S(1)}, u32[]{:S(2)}, u32[]{:S(2)}) collective-permute-start(f32[1,1,32,128]{3,2,1,0:T(8,128)S(1)} %get-tuple-element.78), channel_id=1, source_target_pairs={{0,4},{4,8},{8,12},{1,5},{5,9},{9,13},{2,6},{6,10},{10,14},{3,7},{... | collective-permute-start | bytes 49160 | tf_op jit(solution)/shard_map/ppermute | solution.py:16
  18.8 18.9 %reshape.630 = f32[8,2,16,2,64,2]{5,4,3,2,1,0:T(8,128)} reshape(f32[16,32,128]{2,1,0:T(8,128)} %param.10) | data formatting | bytes 524288 | tf_op jit(solution)/shard_map/reshape | solution.py:75
  37.6 7.0 %reduce_sum.86 = f32[8,16,64]{2,1,0:T(8,128)S(1)} reduce(f32[8,2,16,2,64,2]{5,4,3,2,1,0:T(8,128)} %reshape.630, f32[]{:T(128)} %constant.147.clone.1), dimensions={1,3,5}, to_apply=%region_3.4 | reduce | flops 57344 | bytes 294916 | tf_op jit(solution)/shard_map/reduce_sum | solution.py:76
  56.9 4.9 %collective-permute-start.9 = (f32[1,1,16,64]{3,2,1,0:T(8,128)S(1)}, f32[1,1,16,64]{3,2,1,0:T(8,128)S(1)}, u32[]{:S(2)}, u32[]{:S(2)}) collective-permute-start(f32[1,1,16,64]{3,2,1,0:T(8,128)S(1)} %get-tuple-element.99), channel_id=1, source_target_pairs={{0,4},{4,8},{8,12},{1,5},{5,9},{9,13},{2,6},{6,10},{10,14},{3,7},{... | collective-permute-start | bytes 12296 | tf_op jit(solution)/shard_map/ppermute | solution.py:16
  64.0 4.3 collective-permute-start.5
  69.7 4.3 collective-permute-start.15
  76.0 4.3 collective-permute-start.7
  85.3 18.1 %reshape.629 = f32[8,2,16,2,64,2]{5,4,3,2,1,0:T(8,128)} reshape(f32[1,16,32,128]{3,2,1,0:T(8,128)S(1)} %fusion.94) | data formatting | bytes 524288 | tf_op jit(solution)/shard_map/reshape | solution.py:75
  103.4 7.0 %reduce_sum.85 = f32[8,16,64]{2,1,0:T(8,128)S(1)} reduce(f32[8,2,16,2,64,2]{5,4,3,2,1,0:T(8,128)} %reshape.629, f32[]{:T(128)} %constant.147.clone.1), dimensions={1,3,5}, to_apply=%region_2.3 | reduce | flops 57344 | bytes 294916 | tf_op jit(solution)/shard_map/reduce_sum | solution.py:76
  110.6 4.4 collective-permute-start.11
  131.6 3.8 collective-permute-start.17
  146.2 3.8 collective-permute-start.23
  202.8 3.8 collective-permute-start.39
  210.4 3.8 collective-permute-start.41
  217.6 3.9 collective-permute-start.43
  229.2 3.8 collective-permute-start.45
  236.9 3.9 collective-permute-start.47
  246.5 7.7 %psum.14 = f32[1,256]{1,0:T(1,128)S(1)} all-reduce(f32[1,256]{1,0:T(1,128)S(1)} %bitcast.510), channel_id=1, replica_groups=mesh['group'=2,'space'=4,'src'=4] {'space'}, use_global_device_ids=true, to_apply=%region_8.9 | all-reduce | flops 256 | bytes 2048 | tf_op jit(solution)/shard_map/psum | solution.py:159
  263.4 4.4 collective-permute-start.51
  271.6 18.1 %reshape.636 = f32[8,2,16,2,64,2]{5,4,3,2,1,0:T(8,128)} reshape(f32[1,16,32,128]{3,2,1,0:T(8,128)S(1)} %fusion.55) | data formatting | bytes 524288 | tf_op jit(solution)/shard_map/reshape | solution.py:75
  289.7 7.0 %reduce_sum.91 = f32[8,16,64]{2,1,0:T(8,128)S(1)} reduce(f32[8,2,16,2,64,2]{5,4,3,2,1,0:T(8,128)} %reshape.636, f32[]{:T(128)} %constant.147.clone.1), dimensions={1,3,5}, to_apply=%region_10.11 | reduce | flops 57344 | bytes 294916 | tf_op jit(solution)/shard_map/reduce_sum | solution.py:76
  296.9 3.9 collective-permute-start.53
  304.1 3.8 collective-permute-start.55
  316.8 3.8 collective-permute-start.57
  331.5 3.8 collective-permute-start.61
  388.1 3.8 collective-permute-start.77
  395.5 3.8 collective-permute-start.79
  402.7 3.9 collective-permute-start.81
  413.1 3.8 collective-permute-start.83
  420.7 3.9 collective-permute-start.85
  428.5 3.9 collective-permute-start.87
  437.2 37.6 %all-reduce.46.cloned.1.call-done = f32[16,32,128]{2,1,0:T(8,128)} async-done(((f32[16,32,128]{2,1,0:T(8,128)}), f32[16,32,128]{2,1,0:T(8,128)}) %all-reduce.46.cloned.1.call-update) | async-done | bytes 262160 | tf_op jit(solution)/shard_map/psum | solution.py:172
  (461 shorter events, 243.6 us)
Async XLA Ops:
  7.2 467.7 %all-reduce.46.cloned.1.call-start = ((), (), s32[]{:S(2)}) async-start(), calls=%async_computation | async-start | bytes 524288 | tf_op jit(solution)/shard_map/psum | solution.py:172
  8.0 48.9 %collective-permute-start.2 = (f32[1,1,32,128]{3,2,1,0:T(8,128)S(1)}, f32[1,1,32,128]{3,2,1,0:T(8,128)S(1)}, u32[]{:S(2)}, u32[]{:S(2)}) collective-permute-start(f32[1,1,32,128]{3,2,1,0:T(8,128)S(1)} %get-tuple-element.76), channel_id=1, source_target_pairs={{0,4},{4,8},{8,12},{1,5},{5,9},{9,13},{2,6},{6,10},{10,14},{3,7},{... | collective-permute-start | bytes 49160 | tf_op jit(solution)/shard_map/ppermute | solution.py:16
  10.3 51.5 %collective-permute-start = (f32[1,1,32,128]{3,2,1,0:T(8,128)S(1)}, f32[1,1,32,128]{3,2,1,0:T(8,128)S(1)}, u32[]{:S(2)}, u32[]{:S(2)}) collective-permute-start(f32[1,1,32,128]{3,2,1,0:T(8,128)S(1)} %get-tuple-element.77), channel_id=1, source_target_pairs={{4,0},{8,4},{12,8},{5,1},{9,5},{13,9},{6,2},{10,6},{14,10},{7,3},{... | collective-permute-start | bytes 49160 | tf_op jit(solution)/shard_map/ppermute | solution.py:19
  12.3 50.8 %collective-permute-start.3 = (f32[1,1,32,128]{3,2,1,0:T(8,128)S(1)}, f32[1,1,32,128]{3,2,1,0:T(8,128)S(1)}, u32[]{:S(2)}, u32[]{:S(2)}) collective-permute-start(f32[1,1,32,128]{3,2,1,0:T(8,128)S(1)} %get-tuple-element.78), channel_id=1, source_target_pairs={{0,4},{4,8},{8,12},{1,5},{5,9},{9,13},{2,6},{6,10},{10,14},{3,7},{... | collective-permute-start | bytes 49160 | tf_op jit(solution)/shard_map/ppermute | solution.py:16
  17.5 45.6 %collective-permute-start.1 = (f32[1,1,32,128]{3,2,1,0:T(8,128)S(1)}, f32[1,1,32,128]{3,2,1,0:T(8,128)S(1)}, u32[]{:S(2)}, u32[]{:S(2)}) collective-permute-start(f32[1,1,32,128]{3,2,1,0:T(8,128)S(1)} %get-tuple-element.79), channel_id=1, source_target_pairs={{4,0},{8,4},{12,8},{5,1},{9,5},{13,9},{6,2},{10,6},{14,10},{7,3},{... | collective-permute-start | bytes 49160 | tf_op jit(solution)/shard_map/ppermute | solution.py:19
  44.7 31.3 %collective-permute-start.8 = (f32[1,1,16,64]{3,2,1,0:T(8,128)S(1)}, f32[1,1,16,64]{3,2,1,0:T(8,128)S(1)}, u32[]{:S(2)}, u32[]{:S(2)}) collective-permute-start(f32[1,1,16,64]{3,2,1,0:T(8,128)S(1)} %get-tuple-element.98), channel_id=1, source_target_pairs={{4,0},{8,4},{12,8},{5,1},{9,5},{13,9},{6,2},{10,6},{14,10},{7,3},{... | collective-permute-start | bytes 12296 | tf_op jit(solution)/shard_map/ppermute | solution.py:19
  56.9 23.5 %collective-permute-start.9 = (f32[1,1,16,64]{3,2,1,0:T(8,128)S(1)}, f32[1,1,16,64]{3,2,1,0:T(8,128)S(1)}, u32[]{:S(2)}, u32[]{:S(2)}) collective-permute-start(f32[1,1,16,64]{3,2,1,0:T(8,128)S(1)} %get-tuple-element.99), channel_id=1, source_target_pairs={{0,4},{4,8},{8,12},{1,5},{5,9},{9,13},{2,6},{6,10},{10,14},{3,7},{... | collective-permute-start | bytes 12296 | tf_op jit(solution)/shard_map/ppermute | solution.py:16
  61.8 61.1 %collective-permute-start.14 = (f32[1,1,8,32]{3,2,1,0:T(8,128)}, f32[1,1,8,32]{3,2,1,0:T(8,128)S(1)}, u32[]{:S(2)}, u32[]{:S(2)}) collective-permute-start(f32[1,1,8,32]{3,2,1,0:T(8,128)} %get-tuple-element.118), channel_id=1, source_target_pairs={{4,0},{8,4},{12,8},{5,1},{9,5},{13,9},{6,2},{10,6},{14,10},{7,3},{... | collective-permute-start | bytes 3080 | tf_op jit(solution)/shard_map/ppermute | solution.py:19
  64.0 5.7 %collective-permute-start.5 = (f32[1,1,32,128]{3,2,1,0:T(8,128)S(1)}, f32[1,1,32,128]{3,2,1,0:T(8,128)S(1)}, u32[]{:S(2)}, u32[]{:S(2)}) collective-permute-start(f32[1,1,32,128]{3,2,1,0:T(8,128)S(1)} %get-tuple-element.74), channel_id=1, source_target_pairs={{0,4},{4,8},{8,12},{1,5},{5,9},{9,13},{2,6},{6,10},{10,14},{3,7},{... | collective-permute-start | bytes 49160 | tf_op jit(solution)/shard_map/ppermute | solution.py:16
  68.3 5.6 %collective-permute-start.4 = (f32[1,1,32,128]{3,2,1,0:T(8,128)S(1)}, f32[1,1,32,128]{3,2,1,0:T(8,128)S(1)}, u32[]{:S(2)}, u32[]{:S(2)}) collective-permute-start(f32[1,1,32,128]{3,2,1,0:T(8,128)S(1)} %get-tuple-element.75), channel_id=1, source_target_pairs={{4,0},{8,4},{12,8},{5,1},{9,5},{13,9},{6,2},{10,6},{14,10},{7,3},{... | collective-permute-start | bytes 49160 | tf_op jit(solution)/shard_map/ppermute | solution.py:19
  69.7 54.7 %collective-permute-start.15 = (f32[1,1,8,32]{3,2,1,0:T(8,128)}, f32[1,1,8,32]{3,2,1,0:T(8,128)S(1)}, u32[]{:S(2)}, u32[]{:S(2)}) collective-permute-start(f32[1,1,8,32]{3,2,1,0:T(8,128)} %get-tuple-element.119), channel_id=1, source_target_pairs={{0,4},{4,8},{8,12},{1,5},{5,9},{9,13},{2,6},{6,10},{10,14},{3,7},{... | collective-permute-start | bytes 3080 | tf_op jit(solution)/shard_map/ppermute | solution.py:16
  74.0 69.9 %collective-permute-start.20 = (f32[1,1,4,16]{3,2,1,0:T(4,128)}, f32[1,1,4,16]{3,2,1,0:T(4,128)S(1)}, u32[]{:S(2)}, u32[]{:S(2)}) collective-permute-start(f32[1,1,4,16]{3,2,1,0:T(4,128)} %get-tuple-element.148), channel_id=1, source_target_pairs={{4,0},{8,4},{12,8},{5,1},{9,5},{13,9},{6,2},{10,6},{14,10},{7,3},{... | collective-permute-start | bytes 776 | tf_op jit(solution)/shard_map/ppermute | solution.py:19
  76.0 5.6 %collective-permute-start.7 = (f32[1,1,32,128]{3,2,1,0:T(8,128)S(1)}, f32[1,1,32,128]{3,2,1,0:T(8,128)S(1)}, u32[]{:S(2)}, u32[]{:S(2)}) collective-permute-start(f32[1,1,32,128]{3,2,1,0:T(8,128)S(1)} %get-tuple-element.72), channel_id=1, source_target_pairs={{0,4},{4,8},{8,12},{1,5},{5,9},{9,13},{2,6},{6,10},{10,14},{3,7},{... | collective-permute-start | bytes 49160 | tf_op jit(solution)/shard_map/ppermute | solution.py:16
  110.6 5.7 %collective-permute-start.11 = (f32[1,1,16,64]{3,2,1,0:T(8,128)S(1)}, f32[1,1,16,64]{3,2,1,0:T(8,128)S(1)}, u32[]{:S(2)}, u32[]{:S(2)}) collective-permute-start(f32[1,1,16,64]{3,2,1,0:T(8,128)S(1)} %get-tuple-element.96), channel_id=1, source_target_pairs={{0,4},{4,8},{8,12},{1,5},{5,9},{9,13},{2,6},{6,10},{10,14},{3,7},{... | collective-permute-start | bytes 12296 | tf_op jit(solution)/shard_map/ppermute | solution.py:16
  116.3 27.5 %collective-permute-start.21 = (f32[1,1,4,16]{3,2,1,0:T(4,128)S(1)}, f32[1,1,4,16]{3,2,1,0:T(4,128)S(1)}, u32[]{:S(2)}, u32[]{:S(2)}) collective-permute-start(f32[1,1,4,16]{3,2,1,0:T(4,128)S(1)} %copy-done.45), channel_id=1, source_target_pairs={{0,4},{4,8},{8,12},{1,5},{5,9},{9,13},{2,6},{6,10},{10,14},{3,7},{... | collective-permute-start | bytes 776 | tf_op jit(solution)/shard_map/ppermute | solution.py:16
  131.6 5.2 %collective-permute-start.17 = (f32[1,1,8,32]{3,2,1,0:T(8,128)S(1)}, f32[1,1,8,32]{3,2,1,0:T(8,128)S(1)}, u32[]{:S(2)}, u32[]{:S(2)}) collective-permute-start(f32[1,1,8,32]{3,2,1,0:T(8,128)S(1)} %get-tuple-element.116), channel_id=1, source_target_pairs={{0,4},{4,8},{8,12},{1,5},{5,9},{9,13},{2,6},{6,10},{10,14},{3,7},{... | collective-permute-start | bytes 3080 | tf_op jit(solution)/shard_map/ppermute | solution.py:16
  138.7 5.2 %collective-permute-start.19 = (f32[1,1,8,32]{3,2,1,0:T(8,128)S(1)}, f32[1,1,8,32]{3,2,1,0:T(8,128)S(1)}, u32[]{:S(2)}, u32[]{:S(2)}) collective-permute-start(f32[1,1,8,32]{3,2,1,0:T(8,128)S(1)} %get-tuple-element.114), channel_id=1, source_target_pairs={{0,4},{4,8},{8,12},{1,5},{5,9},{9,13},{2,6},{6,10},{10,14},{3,7},{... | collective-permute-start | bytes 3080 | tf_op jit(solution)/shard_map/ppermute | solution.py:16
  146.2 5.1 %collective-permute-start.23 = (f32[1,1,4,16]{3,2,1,0:T(4,128)S(1)}, f32[1,1,4,16]{3,2,1,0:T(4,128)S(1)}, u32[]{:S(2)}, u32[]{:S(2)}) collective-permute-start(f32[1,1,4,16]{3,2,1,0:T(4,128)S(1)} %get-tuple-element.146), channel_id=1, source_target_pairs={{0,4},{4,8},{8,12},{1,5},{5,9},{9,13},{2,6},{6,10},{10,14},{3,7},{... | collective-permute-start | bytes 776 | tf_op jit(solution)/shard_map/ppermute | solution.py:16
  202.8 5.1 %collective-permute-start.39 = (f32[1,1,8,32]{3,2,1,0:T(8,128)S(1)}, f32[1,1,8,32]{3,2,1,0:T(8,128)S(1)}, u32[]{:S(2)}, u32[]{:S(2)}) collective-permute-start(f32[1,1,8,32]{3,2,1,0:T(8,128)S(1)} %get-tuple-element.108), channel_id=1, source_target_pairs={{0,4},{4,8},{8,12},{1,5},{5,9},{9,13},{2,6},{6,10},{10,14},{3,7},{... | collective-permute-start | bytes 3080 | tf_op jit(solution)/shard_map/ppermute | solution.py:16
  210.4 5.1 %collective-permute-start.41 = (f32[1,1,16,64]{3,2,1,0:T(8,128)S(1)}, f32[1,1,16,64]{3,2,1,0:T(8,128)S(1)}, u32[]{:S(2)}, u32[]{:S(2)}) collective-permute-start(f32[1,1,16,64]{3,2,1,0:T(8,128)S(1)} %get-tuple-element.90), channel_id=1, source_target_pairs={{0,4},{4,8},{8,12},{1,5},{5,9},{9,13},{2,6},{6,10},{10,14},{3,7},{... | collective-permute-start | bytes 12296 | tf_op jit(solution)/shard_map/ppermute | solution.py:16
  217.6 5.2 %collective-permute-start.43 = (f32[1,1,16,64]{3,2,1,0:T(8,128)S(1)}, f32[1,1,16,64]{3,2,1,0:T(8,128)S(1)}, u32[]{:S(2)}, u32[]{:S(2)}) collective-permute-start(f32[1,1,16,64]{3,2,1,0:T(8,128)S(1)} %get-tuple-element.88), channel_id=1, source_target_pairs={{0,4},{4,8},{8,12},{1,5},{5,9},{9,13},{2,6},{6,10},{10,14},{3,7},{... | collective-permute-start | bytes 12296 | tf_op jit(solution)/shard_map/ppermute | solution.py:16
  229.2 5.8 %collective-permute-start.45 = (f32[1,1,32,128]{3,2,1,0:T(8,128)S(1)}, f32[1,1,32,128]{3,2,1,0:T(8,128)S(1)}, u32[]{:S(2)}, u32[]{:S(2)}) collective-permute-start(f32[1,1,32,128]{3,2,1,0:T(8,128)S(1)} %get-tuple-element.70), channel_id=1, source_target_pairs={{0,4},{4,8},{8,12},{1,5},{5,9},{9,13},{2,6},{6,10},{10,14},{3,7},{... | collective-permute-start | bytes 49160 | tf_op jit(solution)/shard_map/ppermute | solution.py:16
  236.9 5.2 %collective-permute-start.47 = (f32[1,1,32,128]{3,2,1,0:T(8,128)S(1)}, f32[1,1,32,128]{3,2,1,0:T(8,128)S(1)}, u32[]{:S(2)}, u32[]{:S(2)}) collective-permute-start(f32[1,1,32,128]{3,2,1,0:T(8,128)S(1)} %get-tuple-element.68), channel_id=1, source_target_pairs={{0,4},{4,8},{8,12},{1,5},{5,9},{9,13},{2,6},{6,10},{10,14},{3,7},{... | collective-permute-start | bytes 49160 | tf_op jit(solution)/shard_map/ppermute | solution.py:16
  263.4 5.9 %collective-permute-start.51 = (f32[1,1,32,128]{3,2,1,0:T(8,128)S(1)}, f32[1,1,32,128]{3,2,1,0:T(8,128)S(1)}, u32[]{:S(2)}, u32[]{:S(2)}) collective-permute-start(f32[1,1,32,128]{3,2,1,0:T(8,128)S(1)} %get-tuple-element.64), channel_id=1, source_target_pairs={{0,4},{4,8},{8,12},{1,5},{5,9},{9,13},{2,6},{6,10},{10,14},{3,7},{... | collective-permute-start | bytes 49160 | tf_op jit(solution)/shard_map/ppermute | solution.py:16
  296.9 5.2 %collective-permute-start.53 = (f32[1,1,16,64]{3,2,1,0:T(8,128)S(1)}, f32[1,1,16,64]{3,2,1,0:T(8,128)S(1)}, u32[]{:S(2)}, u32[]{:S(2)}) collective-permute-start(f32[1,1,16,64]{3,2,1,0:T(8,128)S(1)} %get-tuple-element.86), channel_id=1, source_target_pairs={{0,4},{4,8},{8,12},{1,5},{5,9},{9,13},{2,6},{6,10},{10,14},{3,7},{... | collective-permute-start | bytes 12296 | tf_op jit(solution)/shard_map/ppermute | solution.py:16
  304.1 5.1 %collective-permute-start.55 = (f32[1,1,16,64]{3,2,1,0:T(8,128)S(1)}, f32[1,1,16,64]{3,2,1,0:T(8,128)S(1)}, u32[]{:S(2)}, u32[]{:S(2)}) collective-permute-start(f32[1,1,16,64]{3,2,1,0:T(8,128)S(1)} %get-tuple-element.84), channel_id=1, source_target_pairs={{0,4},{4,8},{8,12},{1,5},{5,9},{9,13},{2,6},{6,10},{10,14},{3,7},{... | collective-permute-start | bytes 12296 | tf_op jit(solution)/shard_map/ppermute | solution.py:16
  316.8 5.2 %collective-permute-start.57 = (f32[1,1,8,32]{3,2,1,0:T(8,128)S(1)}, f32[1,1,8,32]{3,2,1,0:T(8,128)S(1)}, u32[]{:S(2)}, u32[]{:S(2)}) collective-permute-start(f32[1,1,8,32]{3,2,1,0:T(8,128)S(1)} %get-tuple-element.106), channel_id=1, source_target_pairs={{0,4},{4,8},{8,12},{1,5},{5,9},{9,13},{2,6},{6,10},{10,14},{3,7},{... | collective-permute-start | bytes 3080 | tf_op jit(solution)/shard_map/ppermute | solution.py:16
  388.1 5.1 %collective-permute-start.77 = (f32[1,1,8,32]{3,2,1,0:T(8,128)S(1)}, f32[1,1,8,32]{3,2,1,0:T(8,128)S(1)}, u32[]{:S(2)}, u32[]{:S(2)}) collective-permute-start(f32[1,1,8,32]{3,2,1,0:T(8,128)S(1)} %get-tuple-element.100), channel_id=1, source_target_pairs={{0,4},{4,8},{8,12},{1,5},{5,9},{9,13},{2,6},{6,10},{10,14},{3,7},{... | collective-permute-start | bytes 3080 | tf_op jit(solution)/shard_map/ppermute | solution.py:16
  402.7 5.2 %collective-permute-start.81 = (f32[1,1,16,64]{3,2,1,0:T(8,128)S(1)}, f32[1,1,16,64]{3,2,1,0:T(8,128)S(1)}, u32[]{:S(2)}, u32[]{:S(2)}) collective-permute-start(f32[1,1,16,64]{3,2,1,0:T(8,128)S(1)} %get-tuple-element.80), channel_id=1, source_target_pairs={{0,4},{4,8},{8,12},{1,5},{5,9},{9,13},{2,6},{6,10},{10,14},{3,7},{... | collective-permute-start | bytes 12296 | tf_op jit(solution)/shard_map/ppermute | solution.py:16
  413.1 5.2 %collective-permute-start.83 = (f32[1,1,32,128]{3,2,1,0:T(8,128)S(1)}, f32[1,1,32,128]{3,2,1,0:T(8,128)S(1)}, u32[]{:S(2)}, u32[]{:S(2)}) collective-permute-start(f32[1,1,32,128]{3,2,1,0:T(8,128)S(1)} %get-tuple-element.62), channel_id=1, source_target_pairs={{0,4},{4,8},{8,12},{1,5},{5,9},{9,13},{2,6},{6,10},{10,14},{3,7},{... | collective-permute-start | bytes 49160 | tf_op jit(solution)/shard_map/ppermute | solution.py:16
  420.7 5.2 %collective-permute-start.85 = (f32[1,1,32,128]{3,2,1,0:T(8,128)S(1)}, f32[1,1,32,128]{3,2,1,0:T(8,128)S(1)}, u32[]{:S(2)}, u32[]{:S(2)}) collective-permute-start(f32[1,1,32,128]{3,2,1,0:T(8,128)S(1)} %get-tuple-element.60), channel_id=1, source_target_pairs={{0,4},{4,8},{8,12},{1,5},{5,9},{9,13},{2,6},{6,10},{10,14},{3,7},{... | collective-permute-start | bytes 49160 | tf_op jit(solution)/shard_map/ppermute | solution.py:16
  428.5 5.2 %collective-permute-start.87 = (f32[2,1,32,128]{3,2,1,0:T(8,128)S(1)}, f32[2,1,32,128]{3,2,1,0:T(8,128)S(1)}, u32[]{:S(2)}, u32[]{:S(2)}) collective-permute-start(f32[2,1,32,128]{3,2,1,0:T(8,128)S(1)} %get-tuple-element.58), channel_id=1, source_target_pairs={{0,4},{4,8},{8,12},{1,5},{5,9},{9,13},{2,6},{6,10},{10,14},{3,7},{... | collective-permute-start | bytes 98312 | tf_op jit(solution)/shard_map/ppermute | solution.py:16
  (105 other events, 2470.0 us)
Sparse Core Ops, SparseCore 0:
  437.4 37.4 all-reduce.45
where the time goes:
time: 486 us; the launch traced here: 483 us
  starting transfers between devices  225 us (46%)
  waiting for transfers between devices  104 us (21%)
  local copies, waits for them, and re-layouts  79.4 us (16%)
  other arithmetic  45.4 us (9%)
  between operations  21.3 us (4%)
  blocking collectives  7.67 us (2%)
    ppermute x44, starting transfers between devices, padded_2(): lax.ppermute(lax.slice_in_dim(block, block.shape[dim] - width, None, axis...  168 us
    ppermute x44, waiting for transfers between devices, padded_2(): lax.ppermute(lax.slice_in_dim(block, 0, width, axis=dim), axis, backward)  66.6 us
    reshape x7, local copies, waits for them, and re-layouts, coarsen(): array.reshape(leading + (size_x // 2, 2, size_y // 2, 2, size_z // 2, 2))  62.3 us
    ppermute x44, starting transfers between devices, padded_2(): lax.ppermute(lax.slice_in_dim(block, 0, width, axis=dim), axis, backward)  57.3 us
    psum x1, waiting for transfers between devices, body(): gradient = lax.psum(local_terms, 'src')  37.6 us
    reduce_sum x9, other arithmetic, coarsen(): return blocks.mean(axis=(-5, -3, -1))  25.2 us
  transfers between devices with their start and end apart: 89, of which 38 were waited for; matrix products, arithmetic and copies ran while one was open for 14% of the time, Pallas kernels for 0%

commit v1 on v0

--- a/solution.py
+++ b/solution.py
@@ -169,7 +169,24 @@
     stacked = boundary_planes(jnp.concatenate((potential, adjoint), 0), 1)
     stacked = jnp.pad(stacked, ((0, 0), (0, 0), (1, 1), (1, 1)))
     local_terms = pairing(stacked[:sources], stacked[sources:])
-    gradient = lax.psum(local_terms, "src")
+
+    def stacks_all_list(a0):
+        workers = jax.lax.axis_size("src")
+
+        def bench_run(now, met_up):
+            if met_up >= workers:
+                return now
+            return bench_run(
+                now
+                + jax.lax.ppermute(
+                    now, "src", [(hop_no, hop_no ^ met_up) for hop_no in range(workers)]
+                ),
+                2 * met_up,
+            )
+
+        return bench_run(a0, 1)
+
+    gradient = stacks_all_list(local_terms)
     return (potential, misfit, gradient)
 
 

time: 486 us -> 457 us (0.940)
  waiting for transfers between devices: 104 us -> 86.1 us
  between operations: 21.3 us -> 7.94 us
    psum x1 -> x0, waiting for transfers between devices: 37.6 us -> none  [body(): gradient = lax.psum(local_terms, 'src')]
    ppermute x0 -> x2, waiting for transfers between devices: none -> 19.4 us  [bench_run(): jax.lax.ppermute(now, 'src', [(hop_no, hop_no ^ met_up) for hop_no in ran...]
  transfers between devices with their start and end apart: 89 -> 90, of which waited for: 38 -> 39; matrix products, arithmetic and copies ran while one was open for 14% -> 15% of each run, Pallas kernels for 0% -> 0%
where the time goes in v1:
time: 457 us; the launch traced here: 454 us
  starting transfers between devices  229 us (50%)
  waiting for transfers between devices  86.1 us (19%)
  local copies, waits for them, and re-layouts  77.7 us (17%)
  other arithmetic  45.5 us (10%)
  between operations  7.94 us (2%)
  blocking collectives  7.67 us (2%)
    ppermute x44, starting transfers between devices, padded_2(): lax.ppermute(lax.slice_in_dim(block, block.shape[dim] - width, None, axis...  168 us
    ppermute x44, waiting for transfers between devices, padded_2(): lax.ppermute(lax.slice_in_dim(block, 0, width, axis=dim), axis, backward)  66.6 us
    reshape x7, local copies, waits for them, and re-layouts, coarsen(): array.reshape(leading + (size_x // 2, 2, size_y // 2, 2, size_z // 2, 2))  62.3 us
    ppermute x44, starting transfers between devices, padded_2(): lax.ppermute(lax.slice_in_dim(block, 0, width, axis=dim), axis, backward)  57.3 us
    reduce_sum x9, other arithmetic, coarsen(): return blocks.mean(axis=(-5, -3, -1))  25.2 us
    ppermute x2, waiting for transfers between devices, bench_run(): jax.lax.ppermute(now, 'src', [(hop_no, hop_no ^ met_up) for hop_no in ran...  19.4 us
  transfers between devices with their start and end apart: 90, of which 39 were waited for; matrix products, arithmetic and copies ran while one was open for 15% of the time, Pallas kernels for 0%

profile of v1, /device:TPU:0, one launch (start us, length us, event | category | flops | bytes accessed | tf_op | source)
XLA Modules:
  0.0 454.4 jit_solution(1584425331305118795)
XLA Ops:
  5.8 5.1 %collective-permute-start.3 = (f32[1,1,32,128]{3,2,1,0:T(8,128)S(1)}, f32[1,1,32,128]{3,2,1,0:T(8,128)S(1)}, u32[]{:S(2)}, u32[]{:S(2)}) collective-permute-start(f32[1,1,32,128]{3,2,1,0:T(8,128)S(1)} %get-tuple-element.78), channel_id=1, source_target_pairs={{0,4},{4,8},{8,12},{1,5},{5,9},{9,13},{2,6},{6,10},{10,14},{3,7},{... | collective-permute-start | bytes 49160 | tf_op jit(solution)/shard_map/ppermute | solution.py:16
  12.2 18.9 %reshape.630 = f32[8,2,16,2,64,2]{5,4,3,2,1,0:T(8,128)} reshape(f32[16,32,128]{2,1,0:T(8,128)} %param.10) | data formatting | bytes 524288 | tf_op jit(solution)/shard_map/reshape | solution.py:75
  31.1 7.0 %reduce_sum.86 = f32[8,16,64]{2,1,0:T(8,128)S(1)} reduce(f32[8,2,16,2,64,2]{5,4,3,2,1,0:T(8,128)} %reshape.630, f32[]{:T(128)} %constant.147.clone.1), dimensions={1,3,5}, to_apply=%region_3.4 | reduce | flops 57344 | bytes 294916 | tf_op jit(solution)/shard_map/reduce_sum | solution.py:76
  50.3 4.9 %collective-permute-start.9 = (f32[1,1,16,64]{3,2,1,0:T(8,128)S(1)}, f32[1,1,16,64]{3,2,1,0:T(8,128)S(1)}, u32[]{:S(2)}, u32[]{:S(2)}) collective-permute-start(f32[1,1,16,64]{3,2,1,0:T(8,128)S(1)} %get-tuple-element.99), channel_id=1, source_target_pairs={{0,4},{4,8},{8,12},{1,5},{5,9},{9,13},{2,6},{6,10},{10,14},{3,7},{... | collective-permute-start | bytes 12296 | tf_op jit(solution)/shard_map/ppermute | solution.py:16
  57.5 4.3 collective-permute-start.5
  63.1 4.3 collective-permute-start.15
  69.5 4.3 collective-permute-start.7
  78.8 18.1 %reshape.629 = f32[8,2,16,2,64,2]{5,4,3,2,1,0:T(8,128)} reshape(f32[1,16,32,128]{3,2,1,0:T(8,128)S(1)} %fusion.94) | data formatting | bytes 524288 | tf_op jit(solution)/shard_map/reshape | solution.py:75
  96.9 7.0 %reduce_sum.85 = f32[8,16,64]{2,1,0:T(8,128)S(1)} reduce(f32[8,2,16,2,64,2]{5,4,3,2,1,0:T(8,128)} %reshape.629, f32[]{:T(128)} %constant.147.clone.1), dimensions={1,3,5}, to_apply=%region_2.3 | reduce | flops 57344 | bytes 294916 | tf_op jit(solution)/shard_map/reduce_sum | solution.py:76
  104.0 4.4 collective-permute-start.11
  125.0 3.8 collective-permute-start.17
  139.6 3.8 collective-permute-start.23
  196.3 3.8 collective-permute-start.39
  203.8 3.8 collective-permute-start.41
  211.0 3.9 collective-permute-start.43
  222.7 3.8 collective-permute-start.45
  230.4 3.9 collective-permute-start.47
  239.9 7.7 %psum.7 = f32[1,256]{1,0:T(1,128)S(1)} all-reduce(f32[1,256]{1,0:T(1,128)S(1)} %bitcast.510), channel_id=1, replica_groups=mesh['group'=2,'space'=4,'src'=4] {'space'}, use_global_device_ids=true, to_apply=%region_8.9 | all-reduce | flops 256 | bytes 2048 | tf_op jit(solution)/shard_map/psum | solution.py:159
  256.9 4.4 collective-permute-start.51
  265.0 18.1 %reshape.636 = f32[8,2,16,2,64,2]{5,4,3,2,1,0:T(8,128)} reshape(f32[1,16,32,128]{3,2,1,0:T(8,128)S(1)} %fusion.55) | data formatting | bytes 524288 | tf_op jit(solution)/shard_map/reshape | solution.py:75
  283.1 7.0 %reduce_sum.91 = f32[8,16,64]{2,1,0:T(8,128)S(1)} reduce(f32[8,2,16,2,64,2]{5,4,3,2,1,0:T(8,128)} %reshape.636, f32[]{:T(128)} %constant.147.clone.1), dimensions={1,3,5}, to_apply=%region_10.11 | reduce | flops 57344 | bytes 294916 | tf_op jit(solution)/shard_map/reduce_sum | solution.py:76
  290.3 3.9 collective-permute-start.53
  297.6 3.8 collective-permute-start.55
  310.2 3.8 collective-permute-start.57
  381.5 3.8 collective-permute-start.77
  389.0 3.8 collective-permute-start.79
  396.1 3.9 collective-permute-start.81
  406.5 3.8 collective-permute-start.83
  414.2 3.9 collective-permute-start.85
  421.9 3.9 collective-permute-start.87
  431.6 6.4 %collective-permute-done.88 = f32[16,32,128]{2,1,0:T(8,128)S(1)} collective-permute-done((f32[16,32,128]{2,1,0:T(8,128)S(1)}, f32[16,32,128]{2,1,0:T(8,128)S(1)}, u32[]{:S(2)}, u32[]{:S(2)}) %collective-permute-start.88) | collective-permute-done | bytes 262176 | tf_op jit(solution)/shard_map/ppermute | solution.py:181
  440.7 13.0 %collective-permute-done.89 = f32[16,32,128]{2,1,0:T(8,128)S(1)} collective-permute-done((f32[16,32,128]{2,1,0:T(8,128)S(1)}, f32[16,32,128]{2,1,0:T(8,128)S(1)}, u32[]{:S(2)}, u32[]{:S(2)}) %collective-permute-start.89) | collective-permute-done | bytes 262176 | tf_op jit(solution)/shard_map/ppermute | solution.py:181
  (463 shorter events, 250.0 us)
Async XLA Ops:
  1.4 48.9 %collective-permute-start.2 = (f32[1,1,32,128]{3,2,1,0:T(8,128)S(1)}, f32[1,1,32,128]{3,2,1,0:T(8,128)S(1)}, u32[]{:S(2)}, u32[]{:S(2)}) collective-permute-start(f32[1,1,32,128]{3,2,1,0:T(8,128)S(1)} %get-tuple-element.76), channel_id=1, source_target_pairs={{0,4},{4,8},{8,12},{1,5},{5,9},{9,13},{2,6},{6,10},{10,14},{3,7},{... | collective-permute-start | bytes 49160 | tf_op jit(solution)/shard_map/ppermute | solution.py:16
  3.7 51.5 %collective-permute-start = (f32[1,1,32,128]{3,2,1,0:T(8,128)S(1)}, f32[1,1,32,128]{3,2,1,0:T(8,128)S(1)}, u32[]{:S(2)}, u32[]{:S(2)}) collective-permute-start(f32[1,1,32,128]{3,2,1,0:T(8,128)S(1)} %get-tuple-element.77), channel_id=1, source_target_pairs={{4,0},{8,4},{12,8},{5,1},{9,5},{13,9},{6,2},{10,6},{14,10},{7,3},{... | collective-permute-start | bytes 49160 | tf_op jit(solution)/shard_map/ppermute | solution.py:19
  5.8 50.8 %collective-permute-start.3 = (f32[1,1,32,128]{3,2,1,0:T(8,128)S(1)}, f32[1,1,32,128]{3,2,1,0:T(8,128)S(1)}, u32[]{:S(2)}, u32[]{:S(2)}) collective-permute-start(f32[1,1,32,128]{3,2,1,0:T(8,128)S(1)} %get-tuple-element.78), channel_id=1, source_target_pairs={{0,4},{4,8},{8,12},{1,5},{5,9},{9,13},{2,6},{6,10},{10,14},{3,7},{... | collective-permute-start | bytes 49160 | tf_op jit(solution)/shard_map/ppermute | solution.py:16
  10.9 45.7 %collective-permute-start.1 = (f32[1,1,32,128]{3,2,1,0:T(8,128)S(1)}, f32[1,1,32,128]{3,2,1,0:T(8,128)S(1)}, u32[]{:S(2)}, u32[]{:S(2)}) collective-permute-start(f32[1,1,32,128]{3,2,1,0:T(8,128)S(1)} %get-tuple-element.79), channel_id=1, source_target_pairs={{4,0},{8,4},{12,8},{5,1},{9,5},{13,9},{6,2},{10,6},{14,10},{7,3},{... | collective-permute-start | bytes 49160 | tf_op jit(solution)/shard_map/ppermute | solution.py:19
  38.1 31.4 %collective-permute-start.8 = (f32[1,1,16,64]{3,2,1,0:T(8,128)S(1)}, f32[1,1,16,64]{3,2,1,0:T(8,128)S(1)}, u32[]{:S(2)}, u32[]{:S(2)}) collective-permute-start(f32[1,1,16,64]{3,2,1,0:T(8,128)S(1)} %get-tuple-element.98), channel_id=1, source_target_pairs={{4,0},{8,4},{12,8},{5,1},{9,5},{13,9},{6,2},{10,6},{14,10},{7,3},{... | collective-permute-start | bytes 12296 | tf_op jit(solution)/shard_map/ppermute | solution.py:19
  50.3 23.5 %collective-permute-start.9 = (f32[1,1,16,64]{3,2,1,0:T(8,128)S(1)}, f32[1,1,16,64]{3,2,1,0:T(8,128)S(1)}, u32[]{:S(2)}, u32[]{:S(2)}) collective-permute-start(f32[1,1,16,64]{3,2,1,0:T(8,128)S(1)} %get-tuple-element.99), channel_id=1, source_target_pairs={{0,4},{4,8},{8,12},{1,5},{5,9},{9,13},{2,6},{6,10},{10,14},{3,7},{... | collective-permute-start | bytes 12296 | tf_op jit(solution)/shard_map/ppermute | solution.py:16
  55.2 61.1 %collective-permute-start.14 = (f32[1,1,8,32]{3,2,1,0:T(8,128)}, f32[1,1,8,32]{3,2,1,0:T(8,128)S(1)}, u32[]{:S(2)}, u32[]{:S(2)}) collective-permute-start(f32[1,1,8,32]{3,2,1,0:T(8,128)} %get-tuple-element.118), channel_id=1, source_target_pairs={{4,0},{8,4},{12,8},{5,1},{9,5},{13,9},{6,2},{10,6},{14,10},{7,3},{... | collective-permute-start | bytes 3080 | tf_op jit(solution)/shard_map/ppermute | solution.py:19
  57.5 5.7 %collective-permute-start.5 = (f32[1,1,32,128]{3,2,1,0:T(8,128)S(1)}, f32[1,1,32,128]{3,2,1,0:T(8,128)S(1)}, u32[]{:S(2)}, u32[]{:S(2)}) collective-permute-start(f32[1,1,32,128]{3,2,1,0:T(8,128)S(1)} %get-tuple-element.74), channel_id=1, source_target_pairs={{0,4},{4,8},{8,12},{1,5},{5,9},{9,13},{2,6},{6,10},{10,14},{3,7},{... | collective-permute-start | bytes 49160 | tf_op jit(solution)/shard_map/ppermute | solution.py:16
  61.7 5.6 %collective-permute-start.4 = (f32[1,1,32,128]{3,2,1,0:T(8,128)S(1)}, f32[1,1,32,128]{3,2,1,0:T(8,128)S(1)}, u32[]{:S(2)}, u32[]{:S(2)}) collective-permute-start(f32[1,1,32,128]{3,2,1,0:T(8,128)S(1)} %get-tuple-element.75), channel_id=1, source_target_pairs={{4,0},{8,4},{12,8},{5,1},{9,5},{13,9},{6,2},{10,6},{14,10},{7,3},{... | collective-permute-start | bytes 49160 | tf_op jit(solution)/shard_map/ppermute | solution.py:19
  63.1 54.6 %collective-permute-start.15 = (f32[1,1,8,32]{3,2,1,0:T(8,128)}, f32[1,1,8,32]{3,2,1,0:T(8,128)S(1)}, u32[]{:S(2)}, u32[]{:S(2)}) collective-permute-start(f32[1,1,8,32]{3,2,1,0:T(8,128)} %get-tuple-element.119), channel_id=1, source_target_pairs={{0,4},{4,8},{8,12},{1,5},{5,9},{9,13},{2,6},{6,10},{10,14},{3,7},{... | collective-permute-start | bytes 3080 | tf_op jit(solution)/shard_map/ppermute | solution.py:16
  67.4 69.8 %collective-permute-start.20 = (f32[1,1,4,16]{3,2,1,0:T(4,128)}, f32[1,1,4,16]{3,2,1,0:T(4,128)S(1)}, u32[]{:S(2)}, u32[]{:S(2)}) collective-permute-start(f32[1,1,4,16]{3,2,1,0:T(4,128)} %get-tuple-element.148), channel_id=1, source_target_pairs={{4,0},{8,4},{12,8},{5,1},{9,5},{13,9},{6,2},{10,6},{14,10},{7,3},{... | collective-permute-start | bytes 776 | tf_op jit(solution)/shard_map/ppermute | solution.py:19
  69.5 5.6 %collective-permute-start.7 = (f32[1,1,32,128]{3,2,1,0:T(8,128)S(1)}, f32[1,1,32,128]{3,2,1,0:T(8,128)S(1)}, u32[]{:S(2)}, u32[]{:S(2)}) collective-permute-start(f32[1,1,32,128]{3,2,1,0:T(8,128)S(1)} %get-tuple-element.72), channel_id=1, source_target_pairs={{0,4},{4,8},{8,12},{1,5},{5,9},{9,13},{2,6},{6,10},{10,14},{3,7},{... | collective-permute-start | bytes 49160 | tf_op jit(solution)/shard_map/ppermute | solution.py:16
  104.0 5.7 %collective-permute-start.11 = (f32[1,1,16,64]{3,2,1,0:T(8,128)S(1)}, f32[1,1,16,64]{3,2,1,0:T(8,128)S(1)}, u32[]{:S(2)}, u32[]{:S(2)}) collective-permute-start(f32[1,1,16,64]{3,2,1,0:T(8,128)S(1)} %get-tuple-element.96), channel_id=1, source_target_pairs={{0,4},{4,8},{8,12},{1,5},{5,9},{9,13},{2,6},{6,10},{10,14},{3,7},{... | collective-permute-start | bytes 12296 | tf_op jit(solution)/shard_map/ppermute | solution.py:16
  109.8 27.5 %collective-permute-start.21 = (f32[1,1,4,16]{3,2,1,0:T(4,128)S(1)}, f32[1,1,4,16]{3,2,1,0:T(4,128)S(1)}, u32[]{:S(2)}, u32[]{:S(2)}) collective-permute-start(f32[1,1,4,16]{3,2,1,0:T(4,128)S(1)} %copy-done.45), channel_id=1, source_target_pairs={{0,4},{4,8},{8,12},{1,5},{5,9},{9,13},{2,6},{6,10},{10,14},{3,7},{... | collective-permute-start | bytes 776 | tf_op jit(solution)/shard_map/ppermute | solution.py:16
  125.0 5.2 %collective-permute-start.17 = (f32[1,1,8,32]{3,2,1,0:T(8,128)S(1)}, f32[1,1,8,32]{3,2,1,0:T(8,128)S(1)}, u32[]{:S(2)}, u32[]{:S(2)}) collective-permute-start(f32[1,1,8,32]{3,2,1,0:T(8,128)S(1)} %get-tuple-element.116), channel_id=1, source_target_pairs={{0,4},{4,8},{8,12},{1,5},{5,9},{9,13},{2,6},{6,10},{10,14},{3,7},{... | collective-permute-start | bytes 3080 | tf_op jit(solution)/shard_map/ppermute | solution.py:16
  132.1 5.2 %collective-permute-start.19 = (f32[1,1,8,32]{3,2,1,0:T(8,128)S(1)}, f32[1,1,8,32]{3,2,1,0:T(8,128)S(1)}, u32[]{:S(2)}, u32[]{:S(2)}) collective-permute-start(f32[1,1,8,32]{3,2,1,0:T(8,128)S(1)} %get-tuple-element.114), channel_id=1, source_target_pairs={{0,4},{4,8},{8,12},{1,5},{5,9},{9,13},{2,6},{6,10},{10,14},{3,7},{... | collective-permute-start | bytes 3080 | tf_op jit(solution)/shard_map/ppermute | solution.py:16
  139.6 5.1 %collective-permute-start.23 = (f32[1,1,4,16]{3,2,1,0:T(4,128)S(1)}, f32[1,1,4,16]{3,2,1,0:T(4,128)S(1)}, u32[]{:S(2)}, u32[]{:S(2)}) collective-permute-start(f32[1,1,4,16]{3,2,1,0:T(4,128)S(1)} %get-tuple-element.146), channel_id=1, source_target_pairs={{0,4},{4,8},{8,12},{1,5},{5,9},{9,13},{2,6},{6,10},{10,14},{3,7},{... | collective-permute-start | bytes 776 | tf_op jit(solution)/shard_map/ppermute | solution.py:16
  196.3 5.1 %collective-permute-start.39 = (f32[1,1,8,32]{3,2,1,0:T(8,128)S(1)}, f32[1,1,8,32]{3,2,1,0:T(8,128)S(1)}, u32[]{:S(2)}, u32[]{:S(2)}) collective-permute-start(f32[1,1,8,32]{3,2,1,0:T(8,128)S(1)} %get-tuple-element.108), channel_id=1, source_target_pairs={{0,4},{4,8},{8,12},{1,5},{5,9},{9,13},{2,6},{6,10},{10,14},{3,7},{... | collective-permute-start | bytes 3080 | tf_op jit(solution)/shard_map/ppermute | solution.py:16
  211.0 5.2 %collective-permute-start.43 = (f32[1,1,16,64]{3,2,1,0:T(8,128)S(1)}, f32[1,1,16,64]{3,2,1,0:T(8,128)S(1)}, u32[]{:S(2)}, u32[]{:S(2)}) collective-permute-start(f32[1,1,16,64]{3,2,1,0:T(8,128)S(1)} %get-tuple-element.88), channel_id=1, source_target_pairs={{0,4},{4,8},{8,12},{1,5},{5,9},{9,13},{2,6},{6,10},{10,14},{3,7},{... | collective-permute-start | bytes 12296 | tf_op jit(solution)/shard_map/ppermute | solution.py:16
  222.7 5.8 %collective-permute-start.45 = (f32[1,1,32,128]{3,2,1,0:T(8,128)S(1)}, f32[1,1,32,128]{3,2,1,0:T(8,128)S(1)}, u32[]{:S(2)}, u32[]{:S(2)}) collective-permute-start(f32[1,1,32,128]{3,2,1,0:T(8,128)S(1)} %get-tuple-element.70), channel_id=1, source_target_pairs={{0,4},{4,8},{8,12},{1,5},{5,9},{9,13},{2,6},{6,10},{10,14},{3,7},{... | collective-permute-start | bytes 49160 | tf_op jit(solution)/shard_map/ppermute | solution.py:16
  230.4 5.2 %collective-permute-start.47 = (f32[1,1,32,128]{3,2,1,0:T(8,128)S(1)}, f32[1,1,32,128]{3,2,1,0:T(8,128)S(1)}, u32[]{:S(2)}, u32[]{:S(2)}) collective-permute-start(f32[1,1,32,128]{3,2,1,0:T(8,128)S(1)} %get-tuple-element.68), channel_id=1, source_target_pairs={{0,4},{4,8},{8,12},{1,5},{5,9},{9,13},{2,6},{6,10},{10,14},{3,7},{... | collective-permute-start | bytes 49160 | tf_op jit(solution)/shard_map/ppermute | solution.py:16
  256.9 5.9 %collective-permute-start.51 = (f32[1,1,32,128]{3,2,1,0:T(8,128)S(1)}, f32[1,1,32,128]{3,2,1,0:T(8,128)S(1)}, u32[]{:S(2)}, u32[]{:S(2)}) collective-permute-start(f32[1,1,32,128]{3,2,1,0:T(8,128)S(1)} %get-tuple-element.64), channel_id=1, source_target_pairs={{0,4},{4,8},{8,12},{1,5},{5,9},{9,13},{2,6},{6,10},{10,14},{3,7},{... | collective-permute-start | bytes 49160 | tf_op jit(solution)/shard_map/ppermute | solution.py:16
  290.3 5.2 %collective-permute-start.53 = (f32[1,1,16,64]{3,2,1,0:T(8,128)S(1)}, f32[1,1,16,64]{3,2,1,0:T(8,128)S(1)}, u32[]{:S(2)}, u32[]{:S(2)}) collective-permute-start(f32[1,1,16,64]{3,2,1,0:T(8,128)S(1)} %get-tuple-element.86), channel_id=1, source_target_pairs={{0,4},{4,8},{8,12},{1,5},{5,9},{9,13},{2,6},{6,10},{10,14},{3,7},{... | collective-permute-start | bytes 12296 | tf_op jit(solution)/shard_map/ppermute | solution.py:16
  297.6 5.1 %collective-permute-start.55 = (f32[1,1,16,64]{3,2,1,0:T(8,128)S(1)}, f32[1,1,16,64]{3,2,1,0:T(8,128)S(1)}, u32[]{:S(2)}, u32[]{:S(2)}) collective-permute-start(f32[1,1,16,64]{3,2,1,0:T(8,128)S(1)} %get-tuple-element.84), channel_id=1, source_target_pairs={{0,4},{4,8},{8,12},{1,5},{5,9},{9,13},{2,6},{6,10},{10,14},{3,7},{... | collective-permute-start | bytes 12296 | tf_op jit(solution)/shard_map/ppermute | solution.py:16
  310.2 5.2 %collective-permute-start.57 = (f32[1,1,8,32]{3,2,1,0:T(8,128)S(1)}, f32[1,1,8,32]{3,2,1,0:T(8,128)S(1)}, u32[]{:S(2)}, u32[]{:S(2)}) collective-permute-start(f32[1,1,8,32]{3,2,1,0:T(8,128)S(1)} %get-tuple-element.106), channel_id=1, source_target_pairs={{0,4},{4,8},{8,12},{1,5},{5,9},{9,13},{2,6},{6,10},{10,14},{3,7},{... | collective-permute-start | bytes 3080 | tf_op jit(solution)/shard_map/ppermute | solution.py:16
  381.5 5.1 %collective-permute-start.77 = (f32[1,1,8,32]{3,2,1,0:T(8,128)S(1)}, f32[1,1,8,32]{3,2,1,0:T(8,128)S(1)}, u32[]{:S(2)}, u32[]{:S(2)}) collective-permute-start(f32[1,1,8,32]{3,2,1,0:T(8,128)S(1)} %get-tuple-element.100), channel_id=1, source_target_pairs={{0,4},{4,8},{8,12},{1,5},{5,9},{9,13},{2,6},{6,10},{10,14},{3,7},{... | collective-permute-start | bytes 3080 | tf_op jit(solution)/shard_map/ppermute | solution.py:16
  396.1 5.2 %collective-permute-start.81 = (f32[1,1,16,64]{3,2,1,0:T(8,128)S(1)}, f32[1,1,16,64]{3,2,1,0:T(8,128)S(1)}, u32[]{:S(2)}, u32[]{:S(2)}) collective-permute-start(f32[1,1,16,64]{3,2,1,0:T(8,128)S(1)} %get-tuple-element.80), channel_id=1, source_target_pairs={{0,4},{4,8},{8,12},{1,5},{5,9},{9,13},{2,6},{6,10},{10,14},{3,7},{... | collective-permute-start | bytes 12296 | tf_op jit(solution)/shard_map/ppermute | solution.py:16
  406.5 5.2 %collective-permute-start.83 = (f32[1,1,32,128]{3,2,1,0:T(8,128)S(1)}, f32[1,1,32,128]{3,2,1,0:T(8,128)S(1)}, u32[]{:S(2)}, u32[]{:S(2)}) collective-permute-start(f32[1,1,32,128]{3,2,1,0:T(8,128)S(1)} %get-tuple-element.62), channel_id=1, source_target_pairs={{0,4},{4,8},{8,12},{1,5},{5,9},{9,13},{2,6},{6,10},{10,14},{3,7},{... | collective-permute-start | bytes 49160 | tf_op jit(solution)/shard_map/ppermute | solution.py:16
  414.2 5.2 %collective-permute-start.85 = (f32[1,1,32,128]{3,2,1,0:T(8,128)S(1)}, f32[1,1,32,128]{3,2,1,0:T(8,128)S(1)}, u32[]{:S(2)}, u32[]{:S(2)}) collective-permute-start(f32[1,1,32,128]{3,2,1,0:T(8,128)S(1)} %get-tuple-element.60), channel_id=1, source_target_pairs={{0,4},{4,8},{8,12},{1,5},{5,9},{9,13},{2,6},{6,10},{10,14},{3,7},{... | collective-permute-start | bytes 49160 | tf_op jit(solution)/shard_map/ppermute | solution.py:16
  421.9 5.2 %collective-permute-start.87 = (f32[2,1,32,128]{3,2,1,0:T(8,128)S(1)}, f32[2,1,32,128]{3,2,1,0:T(8,128)S(1)}, u32[]{:S(2)}, u32[]{:S(2)}) collective-permute-start(f32[2,1,32,128]{3,2,1,0:T(8,128)S(1)} %get-tuple-element.58), channel_id=1, source_target_pairs={{0,4},{4,8},{8,12},{1,5},{5,9},{9,13},{2,6},{6,10},{10,14},{3,7},{... | collective-permute-start | bytes 98312 | tf_op jit(solution)/shard_map/ppermute | solution.py:16
  429.9 8.0 %collective-permute-start.88 = (f32[16,32,128]{2,1,0:T(8,128)S(1)}, f32[16,32,128]{2,1,0:T(8,128)S(1)}, u32[]{:S(2)}, u32[]{:S(2)}) collective-permute-start(f32[16,32,128]{2,1,0:T(8,128)S(1)} %fusion.21), channel_id=1, source_target_pairs={{0,1},{1,0},{2,3},{3,2},{4,5},{5,4},{6,7},{7,6},{8,9},{9,8},{10,11... | collective-permute-start | bytes 786440 | tf_op jit(solution)/shard_map/ppermute | solution.py:181
  438.0 15.7 %collective-permute-start.89 = (f32[16,32,128]{2,1,0:T(8,128)S(1)}, f32[16,32,128]{2,1,0:T(8,128)S(1)}, u32[]{:S(2)}, u32[]{:S(2)}) collective-permute-start(f32[16,32,128]{2,1,0:T(8,128)S(1)} %add.1628), channel_id=1, source_target_pairs={{0,2},{1,3},{2,0},{3,1},{4,6},{5,7},{6,4},{7,5},{8,10},{9,11},{10,... | collective-permute-start | bytes 786440 | tf_op jit(solution)/shard_map/ppermute | solution.py:181
  (106 other events, 2475.1 us)
